TPU v7x, 256 devices: a whole 4x4x8 slice. The times are simulated.
256 devices in a mesh: orb: 16 (over y, x), aux: 16 (over z, core).
Axes of the slice: x: 4, y: 4, z: 8, core: 2. Of those that a mesh axis runs over, the one named last changes fastest.
Arguments:
- b_rows: bfloat16 [4096, 128, 8, 128], P('aux', 'orb'), may hold values from -6 to 6
- col_blocks: int32 [16, 8], P('orb'), may hold values from 0 to 15, all different within a row
- g_occ: bfloat16 [2, 128, 128], P(None, 'orb'), may hold values from -0.5 to 0.5
- occ_live: int32 [2, 16, 16], replicated, may hold values 0 or 1
- g_virt: bfloat16 [2, 16, 128, 128], P(None, 'orb', 'aux'), may hold values from -0.5 to 0.5
- tau_weight: float32 [2], replicated, may hold values from 0.5 to 2
Outputs:
- chi: float32 [256, 4096], P('orb', 'aux')
Inputs may be any that keep to these rules, and one draw needn't show every extreme that they name: `col_blocks`: each row group lists 8 different column blocks, and every column block is listed by some row group.
All inputs are finite; a program needn't handle non-finite values.
Results may differ from a plain program's by a relative error of at most 0.0041.
Values may be sent and summed in bfloat16 or wider, within the bound.
A program may use at most 128 MiB of HBM per device.

v0:
```python
import math
import jax
import jax.numpy as jnp
from jax import lax
from jax.sharding import PartitionSpec as P


def on_device(b_rows, col_blocks, g_occ, occ_live, g_virt, tau_weight):
    orb_count = lax.axis_size("orb")
    aux_dev, rows_dev, slot_count, tile_width = b_rows.shape
    tau_count = g_occ.shape[0]
    picked = (col_blocks[0][:, None] == jnp.arange(orb_count, dtype=jnp.int32)[None, :]).astype(
        jnp.bfloat16
    )
    outgoing = jnp.einsum("prkc,kd->prdc", b_rows, picked)
    occ_full = lax.all_gather(g_occ, "orb", axis=1, tiled=True)
    total_rows = occ_full.shape[1]
    live_mask = jnp.repeat(jnp.repeat(occ_live, rows_dev, axis=1), rows_dev, axis=2).astype(
        jnp.bfloat16
    )
    occ_masked = occ_full * live_mask
    virt_block = lax.all_gather(g_virt, "aux", axis=2, tiled=True)
    col_dense = lax.all_to_all(outgoing, "orb", split_axis=2, concat_axis=1, tiled=True).reshape(
        aux_dev, total_rows, tile_width
    )
    virt_list = []
    for moment in range(tau_count):
        product = jnp.dot(
            col_dense.reshape(aux_dev * total_rows, tile_width),
            virt_block[moment, 0],
            preferred_element_type=jnp.float32,
        )
        virt_list.append(product.astype(jnp.bfloat16).reshape(aux_dev, total_rows, tile_width))
    partial_value = jnp.zeros((aux_dev, aux_dev), jnp.float32)
    for moment in range(tau_count):
        occ_prod = jnp.einsum(
            "mn,qnc->qmc", occ_masked[moment], col_dense, preferred_element_type=jnp.float32
        ).astype(jnp.bfloat16)
        term = jnp.einsum(
            "pmc,qmc->qp", virt_list[moment], occ_prod, preferred_element_type=jnp.float32
        )
        partial_value = partial_value + tau_weight[moment] * term
    partial_value = partial_value * (1.0 / math.sqrt(total_rows * tile_width * orb_count))
    whole_sum = lax.psum(partial_value, "orb")
    share_rows = aux_dev // orb_count
    share = lax.dynamic_slice_in_dim(whole_sum, lax.axis_index("orb") * share_rows, share_rows, 0)
    return share


def solution(mesh):
    in_specs = (
        P("aux", "orb", None, None),
        P("orb", None),
        P(None, "orb", None),
        P(),
        P(None, "orb", "aux", None),
        P(),
    )
    out_specs = P("orb", "aux")
    return jax.shard_map(
        on_device, mesh=mesh, in_specs=in_specs, out_specs=out_specs, check_vma=False
    )
```

profile of v0, /device:TPU:2, one launch (start us, length us, event | category | flops | bytes accessed | tf_op | source)
XLA Modules:
  0.0 368.9 jit_solution(9843376873879229038)
XLA Ops:
  6.5 6.3 %convolution_bitcast_fusion = bf16[256,8,16,128]{3,2,1,0:T(8,128)(2,1)} fusion(bf16[256,8,8,128]{3,2,1,0:T(8,128)(2,1)} %param.6, s32[8]{0:T(128)} %bitcast.83), kind=kOutput, calls=%fused_computation.8 | convolution fusion | flops 67108992 | bytes 12582944 | tf_op jit(solution)/shard_map/prkc,kd->prdc/dot_general | solution.py:15
  12.8 8.8 %copy.23 = bf16[256,8,16,128]{3,1,0,2:T(8,128)(2,1)} copy(bf16[256,8,16,128]{3,2,1,0:T(8,128)(2,1)} %convolution_bitcast_fusion) | data formatting | bytes 16777216 | tf_op jit(solution)/shard_map/prkc,kd->prdc/transpose | solution.py:15
  21.6 0.0 copy-start.1
  21.6 0.0 copy-start.2
  21.6 0.0 copy-start.3
  21.6 0.0 copy-start.4
  21.6 7.6 %all-to-all-start = ((bf16[256,8,16,128]{3,1,0,2:T(8,128)(2,1)}), bf16[256,8,16,128]{3,1,0,2:T(8,128)(2,1)}, u32[]{:S(2)}, u32[]{:S(2)}) async-start(bf16[256,8,16,128]{3,1,0,2:T(8,128)(2,1)} %copy.23), calls=%async_computation | async-start | bytes 16777216 | tf_op jit(solution)/shard_map/all_to_all | solution.py:23
  29.2 0.0 all-reduce.2.cloned.1.call-start
  29.3 0.0 copy-done.1
  29.3 0.1 copy.25
  29.4 0.1 copy.26
  29.5 0.0 copy-done.2
  29.5 137.6 %all_gather.6 = bf16[2,128,128]{2,1,0:T(8,128)(2,1)S(1)} all-gather(bf16[2,8,128]{2,1,0:T(8,128)(2,1)S(1)} %copy-done.2), channel_id=1, replica_groups=mesh['orb'=16,'aux'=16] {'orb'}, dimensions={1}, use_global_device_ids=true | all-gather | bytes 69632 | tf_op jit(solution)/shard_map/all_gather | solution.py:16
  167.1 0.0 copy-done.3
  167.2 20.1 %all_gather.7 = bf16[2,1,128,128]{3,2,1,0:T(8,128)(2,1)S(1)} all-gather(bf16[2,1,8,128]{3,2,1,0:T(8,128)(2,1)S(1)} %copy-done.3), channel_id=1, replica_groups=mesh['orb'=16,'aux'=16] {'aux'}, dimensions={2}, use_global_device_ids=true | all-gather | bytes 69632 | tf_op jit(solution)/shard_map/all_gather | solution.py:22
  187.3 0.0 copy-done.4
  187.3 0.6 fusion.31
  187.9 0.0 all-to-all-done
  187.9 9.0 %copy.34 = bf16[256,8,16,128]{3,1,2,0:T(8,128)(2,1)} copy(bf16[256,8,16,128]{3,1,0,2:T(8,128)(2,1)} %all-to-all-done) | data formatting | bytes 16777216 | tf_op jit(solution)/shard_map/all_to_all | solution.py:23
  196.9 0.0 copy-start
  196.9 9.1 %convolution_convert_fusion = bf16[32768,128]{1,0:T(8,128)(2,1)} fusion(bf16[32768,128]{1,0:T(8,128)(2,1)} %bitcast.78, bf16[2,1,128,128]{3,2,1,0:T(8,128)(2,1)S(1)} %all_gather.7), kind=kOutput, calls=%fused_computation | convolution fusion | flops 1077936128 | bytes 16809984 | tf_op jit(solution)/shard_map/dot_general | solution.py:28
  206.0 0.0 copy-done
  206.0 4.5 %convolution_convert_fusion.1 = bf16[32768,128]{1,0:T(8,128)(2,1)} fusion(bf16[32768,128]{1,0:T(8,128)(2,1)S(1)} %bitcast.80, bf16[2,1,128,128]{3,2,1,0:T(8,128)(2,1)S(1)} %all_gather.7), kind=kOutput, calls=%fused_computation.1 | convolution fusion | flops 1077936128 | bytes 16809984 | tf_op jit(solution)/shard_map/dot_general | solution.py:28
  210.5 11.8 %copy.30 = bf16[256,128,128]{1,0,2:T(8,128)(2,1)} copy(bf16[256,128,128]{2,1,0:T(8,128)(2,1)} %bitcast.82) | data formatting | bytes 16777216 | tf_op jit(solution)/shard_map/reshape | solution.py:33
  222.3 11.8 %copy.27 = bf16[256,128,128]{1,0,2:T(8,128)(2,1)} copy(bf16[256,128,128]{2,1,0:T(8,128)(2,1)} %bitcast.79) | data formatting | bytes 16777216 | tf_op jit(solution)/shard_map/reshape | solution.py:23
  234.1 12.3 %copy.28 = bf16[256,128,128]{1,0,2:T(8,128)(2,1)} copy(bf16[256,128,128]{2,1,0:T(8,128)(2,1)} %bitcast.81) | data formatting | bytes 16777216 | tf_op jit(solution)/shard_map/reshape | solution.py:33
  246.4 11.0 %fusion.16 = f32[256,256]{1,0:T(8,128)S(1)} fusion(bf16[256,128,128]{1,0,2:T(8,128)(2,1)} %copy.30, bf16[256,128,128]{1,0,2:T(8,128)(2,1)} %copy.27, f32[]{:T(128)} %bitcast.18, bf16[2,128,128]{2,1,0:T(8,128)(2,1)S(1)} %mul.25), kind=kOutput, calls=%fused_computation.13 | convolution fusion | flops 3225485312 | bytes 17072132 | tf_op jit(solution)/shard_map/pmc,qmc->qp/dot_general | solution.py:39
  257.5 11.8 %fusion.25 = f32[256,256]{1,0:T(8,128)} fusion(f32[256,256]{1,0:T(8,128)S(1)} %fusion.16, bf16[256,128,128]{1,0,2:T(8,128)(2,1)} %copy.28, bf16[256,128,128]{1,0,2:T(8,128)(2,1)} %copy.27, f32[]{:T(128)} %bitcast, bf16[2,128,128]{2,1,0:T(8,128)(2,1)S(1)} %mul.25), kind=kOutput, calls=%fused_computation.16 | convolution fusion | flops 3225616384 | bytes 17334276 | tf_op jit(solution)/shard_map/pmc,qmc->qp/dot_general | solution.py:39
  269.3 0.0 all-reduce.2.cloned.1.call-update
  269.3 91.4 %all-reduce.2.cloned.1.call-done = f32[256,256]{1,0:T(8,128)} async-done(((f32[256,256]{1,0:T(8,128)}), f32[256,256]{1,0:T(8,128)}) %all-reduce.2.cloned.1.call-update) | async-done | bytes 262160 | tf_op jit(solution)/shard_map/psum | solution.py:44
  360.7 1.3 constant_dynamic-slice_fusion
  (4 shorter events, 0.1 us)
Async XLA Ops:
  21.6 7.7 %copy-start.1 = (s32[2,16,16]{2,1,0:T(8,128)S(1)}, s32[2,16,16]{2,1,0:T(8,128)}, u32[]{:S(2)}) copy-start(s32[2,16,16]{2,1,0:T(8,128)} %param.9) | copy-start | bytes 6148
  21.6 8.0 %copy-start.2 = (bf16[2,8,128]{2,1,0:T(8,128)(2,1)S(1)}, bf16[2,8,128]{2,1,0:T(8,128)(2,1)}, u32[]{:S(2)}) copy-start(bf16[2,8,128]{2,1,0:T(8,128)(2,1)} %param.8) | copy-start | bytes 12292
  21.6 145.6 %copy-start.3 = (bf16[2,1,8,128]{3,2,1,0:T(8,128)(2,1)S(1)}, bf16[2,1,8,128]{3,2,1,0:T(8,128)(2,1)}, u32[]{:S(2)}) copy-start(bf16[2,1,8,128]{3,2,1,0:T(8,128)(2,1)} %param.10) | copy-start | bytes 12292
  21.6 165.7 %copy-start.4 = (f32[2]{0:T(128)S(1)}, f32[2]{0:T(128)}, u32[]{:S(2)}) copy-start(f32[2]{0:T(128)} %param.11) | copy-start | bytes 28
  21.6 166.3 %all-to-all-start = ((bf16[256,8,16,128]{3,1,0,2:T(8,128)(2,1)}), bf16[256,8,16,128]{3,1,0,2:T(8,128)(2,1)}, u32[]{:S(2)}, u32[]{:S(2)}) async-start(bf16[256,8,16,128]{3,1,0,2:T(8,128)(2,1)} %copy.23), calls=%async_computation | async-start | bytes 16777216 | tf_op jit(solution)/shard_map/all_to_all | solution.py:23
  29.2 331.5 %all-reduce.2.cloned.1.call-start = ((), (), s32[]{:S(2)}) async-start(), calls=%async_computation.1 | async-start | bytes 524288 | tf_op jit(solution)/shard_map/psum | solution.py:44
  196.9 9.1 %copy-start = (bf16[256,8,16,128]{3,1,2,0:T(8,128)(2,1)S(1)}, bf16[256,8,16,128]{3,1,2,0:T(8,128)(2,1)}, u32[]{:S(2)}) copy-start(bf16[256,8,16,128]{3,1,2,0:T(8,128)(2,1)} %copy.34) | copy-start | bytes 25165828
Sparse Core Ops, SparseCore 0:
  269.4 91.2 all-reduce.1
where the time goes:
time: 370 us; the launch traced here: 369 us
  blocking collectives  158 us (43%)
  waiting for transfers between devices  91.4 us (25%)
  local copies, waits for them, and re-layouts  55.9 us (15%)
  matrix products  42.7 us (12%)
  between operations  13.5 us (4%)
  starting transfers between devices  7.66 us (2%)
    all_gather x1, blocking collectives, on_device(): occ_full = lax.all_gather(g_occ, 'orb', axis=1, tiled=True)  138 us
    psum x1, waiting for transfers between devices, on_device(): whole_sum = lax.psum(partial_value, 'orb')  91.4 us
    reshape x2, local copies, waits for them, and re-layouts, on_device(): product.astype(jnp.bfloat16).reshape(aux_dev, total_rows, tile_width)  24.1 us
    dot_general x2, matrix products, on_device(): jnp.einsum('pmc,qmc->qp', virt_list[moment], occ_prod, preferred_element_...  22.9 us
    all_gather x1, blocking collectives, on_device(): virt_block = lax.all_gather(g_virt, 'aux', axis=2, tiled=True)  20.1 us
    dot_general x2, matrix products, on_device(): jnp.dot(col_dense.reshape(aux_dev * total_rows, tile_width), virt_block[m...  13.6 us
    reshape x1, local copies, waits for them, and re-layouts, on_device(): lax.all_to_all(outgoing, 'orb', split_axis=2, concat_axis=1, tiled=True)  11.8 us
    all_to_all x1, local copies, waits for them, and re-layouts, on_device(): lax.all_to_all(outgoing, 'orb', split_axis=2, concat_axis=1, tiled=True)  9.03 us
  transfers between devices with their start and end apart: 2, of which 1 were waited for; matrix products, arithmetic and copies ran while one was open for 0% of the time, Pallas kernels for 0%

commit v1 on v0

--- a/solution.py
+++ b/solution.py
@@ -3,6 +3,14 @@
 import jax.numpy as jnp
 from jax import lax
 from jax.sharding import PartitionSpec as P
+
+
+def add_in_pairs(block, mesh_axis):
+    size, summed = (lax.axis_size(mesh_axis), block)
+    for reach in [1 << k for k in range(size.bit_length() - 1)]:
+        route = [(i, i ^ reach) for i in range(size)]
+        summed = summed + lax.ppermute(summed, mesh_axis, route)
+    return summed
 
 
 def on_device(b_rows, col_blocks, g_occ, occ_live, g_virt, tau_weight):
@@ -41,7 +49,7 @@
         )
         partial_value = partial_value + tau_weight[moment] * term
     partial_value = partial_value * (1.0 / math.sqrt(total_rows * tile_width * orb_count))
-    whole_sum = lax.psum(partial_value, "orb")
+    whole_sum = add_in_pairs(partial_value, "orb")
     share_rows = aux_dev // orb_count
     share = lax.dynamic_slice_in_dim(whole_sum, lax.axis_index("orb") * share_rows, share_rows, 0)
     return share

time: 370 us -> 296 us (0.80)
  waiting for transfers between devices: 91.4 us -> 25.8 us
  between operations: 13.5 us -> 0.1 us
  starting transfers between devices: 7.66 us -> 14.6 us
    psum x1 -> x0, waiting for transfers between devices: 91.4 us -> none  [on_device(): whole_sum = lax.psum(partial_value, 'orb')]
    ppermute x0 -> x4, waiting for transfers between devices: none -> 25.8 us  [add_in_pairs(): summed = summed + lax.ppermute(summed, mesh_axis, route)]
    ppermute x0 -> x4, starting transfers between devices: none -> 7.03 us  [add_in_pairs(): summed = summed + lax.ppermute(summed, mesh_axis, route)]
  transfers between devices with their start and end apart: 2 -> 5, of which waited for: 1 -> 4; matrix products, arithmetic and copies ran while one was open for 0% -> 0% of each run, Pallas kernels for 0% -> 0%
where the time goes in v1:
time: 296 us; the launch traced here: 295 us
  blocking collectives  158 us (53%)
  local copies, waits for them, and re-layouts  53.9 us (18%)
  matrix products  41.9 us (14%)
  waiting for transfers between devices  25.8 us (9%)
  starting transfers between devices  14.6 us (5%)
    all_gather x1, blocking collectives, on_device(): occ_full = lax.all_gather(g_occ, 'orb', axis=1, tiled=True)  138 us
    ppermute x4, waiting for transfers between devices, add_in_pairs(): summed = summed + lax.ppermute(summed, mesh_axis, route)  25.8 us
    reshape x2, local copies, waits for them, and re-layouts, on_device(): product.astype(jnp.bfloat16).reshape(aux_dev, total_rows, tile_width)  23.6 us
    dot_general x2, matrix products, on_device(): jnp.einsum('pmc,qmc->qp', virt_list[moment], occ_prod, preferred_element_...  22.1 us
    all_gather x1, blocking collectives, on_device(): virt_block = lax.all_gather(g_virt, 'aux', axis=2, tiled=True)  20.1 us
    dot_general x2, matrix products, on_device(): jnp.dot(col_dense.reshape(aux_dev * total_rows, tile_width), virt_block[m...  13.5 us
    reshape x1, local copies, waits for them, and re-layouts, on_device(): lax.all_to_all(outgoing, 'orb', split_axis=2, concat_axis=1, tiled=True)  11.7 us
    all_to_all x1, local copies, waits for them, and re-layouts, on_device(): lax.all_to_all(outgoing, 'orb', split_axis=2, concat_axis=1, tiled=True)  9.01 us
  transfers between devices with their start and end apart: 5, of which 4 were waited for; matrix products, arithmetic and copies ran while one was open for 0% of the time, Pallas kernels for 0%

profile of v1, /device:TPU:2, one launch (start us, length us, event | category | flops | bytes accessed | tf_op | source)
XLA Modules:
  0.0 294.9 jit_solution(8986897087281383094)
XLA Ops:
  0.0 6.3 %convolution_bitcast_fusion = bf16[256,8,16,128]{3,2,1,0:T(8,128)(2,1)} fusion(bf16[256,8,8,128]{3,2,1,0:T(8,128)(2,1)} %param.6, s32[8]{0:T(128)} %bitcast.83), kind=kOutput, calls=%fused_computation.8 | convolution fusion | flops 67108992 | bytes 12582944 | tf_op jit(solution)/shard_map/prkc,kd->prdc/dot_general | solution.py:23
  6.3 8.8 %copy.23 = bf16[256,8,16,128]{3,1,0,2:T(8,128)(2,1)} copy(bf16[256,8,16,128]{3,2,1,0:T(8,128)(2,1)} %convolution_bitcast_fusion) | data formatting | bytes 16777216 | tf_op jit(solution)/shard_map/prkc,kd->prdc/transpose | solution.py:23
  15.0 0.0 copy-start.1
  15.0 7.6 %all-to-all-start = ((bf16[256,8,16,128]{3,1,0,2:T(8,128)(2,1)}), bf16[256,8,16,128]{3,1,0,2:T(8,128)(2,1)}, u32[]{:S(2)}, u32[]{:S(2)}) async-start(bf16[256,8,16,128]{3,1,0,2:T(8,128)(2,1)} %copy.23), calls=%async_computation | async-start | bytes 16777216 | tf_op jit(solution)/shard_map/all_to_all | solution.py:31
  22.6 0.0 copy-done.1
  22.7 0.1 copy.25
  22.8 0.1 copy.26
  22.9 0.0 copy-done.2
  22.9 137.6 %all_gather.6 = bf16[2,128,128]{2,1,0:T(8,128)(2,1)S(1)} all-gather(bf16[2,8,128]{2,1,0:T(8,128)(2,1)S(1)} %copy-done.2), channel_id=1, replica_groups=mesh['orb'=16,'aux'=16] {'orb'}, dimensions={1}, use_global_device_ids=true | all-gather | bytes 69632 | tf_op jit(solution)/shard_map/all_gather | solution.py:24
  160.6 0.0 copy-done.3
  160.6 20.1 %all_gather.7 = bf16[2,1,128,128]{3,2,1,0:T(8,128)(2,1)S(1)} all-gather(bf16[2,1,8,128]{3,2,1,0:T(8,128)(2,1)S(1)} %copy-done.3), channel_id=1, replica_groups=mesh['orb'=16,'aux'=16] {'aux'}, dimensions={2}, use_global_device_ids=true | all-gather | bytes 69632 | tf_op jit(solution)/shard_map/all_gather | solution.py:30
  180.7 0.0 copy-done.4
  180.8 0.6 fusion.31
  181.3 0.0 all-to-all-done
  181.3 9.0 %copy.34 = bf16[256,8,16,128]{3,1,2,0:T(8,128)(2,1)} copy(bf16[256,8,16,128]{3,1,0,2:T(8,128)(2,1)} %all-to-all-done) | data formatting | bytes 16777216 | tf_op jit(solution)/shard_map/all_to_all | solution.py:31
  190.4 9.1 %convolution_convert_fusion = bf16[32768,128]{1,0:T(8,128)(2,1)} fusion(bf16[32768,128]{1,0:T(8,128)(2,1)} %bitcast.78, bf16[2,1,128,128]{3,2,1,0:T(8,128)(2,1)S(1)} %all_gather.7), kind=kOutput, calls=%fused_computation | convolution fusion | flops 1077936128 | bytes 16809984 | tf_op jit(solution)/shard_map/dot_general | solution.py:36
  199.4 0.0 copy-done
  199.4 4.5 %convolution_convert_fusion.1 = bf16[32768,128]{1,0:T(8,128)(2,1)} fusion(bf16[32768,128]{1,0:T(8,128)(2,1)S(1)} %bitcast.80, bf16[2,1,128,128]{3,2,1,0:T(8,128)(2,1)S(1)} %all_gather.7), kind=kOutput, calls=%fused_computation.1 | convolution fusion | flops 1077936128 | bytes 16809984 | tf_op jit(solution)/shard_map/dot_general | solution.py:36
  203.9 11.8 %copy.30 = bf16[256,128,128]{1,0,2:T(8,128)(2,1)} copy(bf16[256,128,128]{2,1,0:T(8,128)(2,1)} %bitcast.82) | data formatting | bytes 16777216 | tf_op jit(solution)/shard_map/reshape | solution.py:41
  215.7 11.7 %copy.27 = bf16[256,128,128]{1,0,2:T(8,128)(2,1)} copy(bf16[256,128,128]{2,1,0:T(8,128)(2,1)} %bitcast.79) | data formatting | bytes 16777216 | tf_op jit(solution)/shard_map/reshape | solution.py:31
  227.5 11.8 %copy.28 = bf16[256,128,128]{1,0,2:T(8,128)(2,1)} copy(bf16[256,128,128]{2,1,0:T(8,128)(2,1)} %bitcast.81) | data formatting | bytes 16777216 | tf_op jit(solution)/shard_map/reshape | solution.py:41
  239.2 11.0 %fusion.16 = f32[256,256]{1,0:T(8,128)S(1)} fusion(bf16[256,128,128]{1,0,2:T(8,128)(2,1)} %copy.30, bf16[256,128,128]{1,0,2:T(8,128)(2,1)} %copy.27, f32[]{:T(128)} %bitcast.18, bf16[2,128,128]{2,1,0:T(8,128)(2,1)S(1)} %mul.25), kind=kOutput, calls=%fused_computation.13 | convolution fusion | flops 3225485312 | bytes 17072132 | tf_op jit(solution)/shard_map/pmc,qmc->qp/dot_general | solution.py:47
  250.2 11.1 %fusion.25 = f32[256,256]{1,0:T(8,128)S(1)} fusion(f32[256,256]{1,0:T(8,128)S(1)} %fusion.16, bf16[256,128,128]{1,0,2:T(8,128)(2,1)} %copy.28, bf16[256,128,128]{1,0,2:T(8,128)(2,1)} %copy.27, f32[]{:T(128)} %bitcast, bf16[2,128,128]{2,1,0:T(8,128)(2,1)S(1)} %mul.25), kind=kOutput, calls=%fused_computation.16 | convolution fusion | flops 3225616384 | bytes 17334276 | tf_op jit(solution)/shard_map/pmc,qmc->qp/dot_general | solution.py:47
  261.3 0.8 collective-permute-start
  262.2 7.8 %collective-permute-done = f32[256,256]{1,0:T(8,128)S(1)} collective-permute-done((f32[256,256]{1,0:T(8,128)S(1)}, f32[256,256]{1,0:T(8,128)S(1)}, u32[]{:S(2)}, u32[]{:S(2)}) %collective-permute-start) | collective-permute-done | bytes 262176 | tf_op jit(solution)/shard_map/ppermute | solution.py:12
  270.0 2.2 collective-permute-start.1
  272.1 7.2 %collective-permute-done.1 = f32[256,256]{1,0:T(8,128)S(1)} collective-permute-done((f32[256,256]{1,0:T(8,128)S(1)}, f32[256,256]{1,0:T(8,128)S(1)}, u32[]{:S(2)}, u32[]{:S(2)}) %collective-permute-start.1) | collective-permute-done | bytes 262176 | tf_op jit(solution)/shard_map/ppermute | solution.py:12
  279.4 1.3 collective-permute-start.2
  280.6 5.6 %collective-permute-done.2 = f32[256,256]{1,0:T(8,128)S(1)} collective-permute-done((f32[256,256]{1,0:T(8,128)S(1)}, f32[256,256]{1,0:T(8,128)S(1)}, u32[]{:S(2)}, u32[]{:S(2)}) %collective-permute-start.2) | collective-permute-done | bytes 262176 | tf_op jit(solution)/shard_map/ppermute | solution.py:12
  286.3 2.8 collective-permute-start.3
  289.1 5.2 %collective-permute-done.3 = f32[256,256]{1,0:T(8,128)S(1)} collective-permute-done((f32[256,256]{1,0:T(8,128)S(1)}, f32[256,256]{1,0:T(8,128)S(1)}, u32[]{:S(2)}, u32[]{:S(2)}) %collective-permute-start.3) | collective-permute-done | bytes 262176 | tf_op jit(solution)/shard_map/ppermute | solution.py:12
  294.3 0.6 dynamic-slice_add_fusion
  (11 shorter events, 0.2 us)
Async XLA Ops:
  15.0 7.6 %copy-start.1 = (s32[2,16,16]{2,1,0:T(8,128)S(1)}, s32[2,16,16]{2,1,0:T(8,128)}, u32[]{:S(2)}) copy-start(s32[2,16,16]{2,1,0:T(8,128)} %param.9) | copy-start | bytes 6148
  15.0 7.9 %copy-start.2 = (bf16[2,8,128]{2,1,0:T(8,128)(2,1)S(1)}, bf16[2,8,128]{2,1,0:T(8,128)(2,1)}, u32[]{:S(2)}) copy-start(bf16[2,8,128]{2,1,0:T(8,128)(2,1)} %param.8) | copy-start | bytes 12292
  15.0 145.6 %copy-start.3 = (bf16[2,1,8,128]{3,2,1,0:T(8,128)(2,1)S(1)}, bf16[2,1,8,128]{3,2,1,0:T(8,128)(2,1)}, u32[]{:S(2)}) copy-start(bf16[2,1,8,128]{3,2,1,0:T(8,128)(2,1)} %param.10) | copy-start | bytes 12292
  15.0 165.7 %copy-start.4 = (f32[2]{0:T(128)S(1)}, f32[2]{0:T(128)}, u32[]{:S(2)}) copy-start(f32[2]{0:T(128)} %param.11) | copy-start | bytes 28
  15.0 166.3 %all-to-all-start = ((bf16[256,8,16,128]{3,1,0,2:T(8,128)(2,1)}), bf16[256,8,16,128]{3,1,0,2:T(8,128)(2,1)}, u32[]{:S(2)}, u32[]{:S(2)}) async-start(bf16[256,8,16,128]{3,1,0,2:T(8,128)(2,1)} %copy.23), calls=%async_computation | async-start | bytes 16777216 | tf_op jit(solution)/shard_map/all_to_all | solution.py:31
  190.4 9.1 %copy-start = (bf16[256,8,16,128]{3,1,2,0:T(8,128)(2,1)S(1)}, bf16[256,8,16,128]{3,1,2,0:T(8,128)(2,1)}, u32[]{:S(2)}) copy-start(bf16[256,8,16,128]{3,1,2,0:T(8,128)(2,1)} %copy.34) | copy-start | bytes 25165828
  261.3 8.6 %collective-permute-start = (f32[256,256]{1,0:T(8,128)S(1)}, f32[256,256]{1,0:T(8,128)S(1)}, u32[]{:S(2)}, u32[]{:S(2)}) collective-permute-start(f32[256,256]{1,0:T(8,128)S(1)} %fusion.25), channel_id=1, source_target_pairs={{0,16},{16,0},{32,48},{48,32},{64,80},{80,64},{96,112},{112,96},{1... | collective-permute-start | bytes 786440 | tf_op jit(solution)/shard_map/ppermute | solution.py:12
  270.0 9.3 %collective-permute-start.1 = (f32[256,256]{1,0:T(8,128)S(1)}, f32[256,256]{1,0:T(8,128)S(1)}, u32[]{:S(2)}, u32[]{:S(2)}) collective-permute-start(f32[256,256]{1,0:T(8,128)S(1)} %add.19), channel_id=1, source_target_pairs={{0,32},{16,48},{32,0},{48,16},{64,96},{80,112},{96,64},{112,80},{1... | collective-permute-start | bytes 786440 | tf_op jit(solution)/shard_map/ppermute | solution.py:12
  279.4 6.9 %collective-permute-start.2 = (f32[256,256]{1,0:T(8,128)S(1)}, f32[256,256]{1,0:T(8,128)S(1)}, u32[]{:S(2)}, u32[]{:S(2)}) collective-permute-start(f32[256,256]{1,0:T(8,128)S(1)} %add.20), channel_id=1, source_target_pairs={{0,64},{16,80},{32,96},{48,112},{64,0},{80,16},{96,32},{112,48},{1... | collective-permute-start | bytes 786440 | tf_op jit(solution)/shard_map/ppermute | solution.py:12
  286.3 8.0 %collective-permute-start.3 = (f32[256,256]{1,0:T(8,128)S(1)}, f32[256,256]{1,0:T(8,128)S(1)}, u32[]{:S(2)}, u32[]{:S(2)}) collective-permute-start(f32[256,256]{1,0:T(8,128)S(1)} %add.21), channel_id=1, source_target_pairs={{0,128},{16,144},{32,160},{48,176},{64,192},{80,208},{96,224},{112... | collective-permute-start | bytes 786440 | tf_op jit(solution)/shard_map/ppermute | solution.py:12
